TPU v7x, 32 devices: a whole 2x2x4 slice. The times are simulated.
32 devices in a mesh: groups: 2 (over y), tm: 4 (over z), cuts: 2 (over x), col: 2 (over core).
Axes of the slice: x: 2, y: 2, z: 4, core: 2. Of those that a mesh axis runs over, the one named last changes fastest.
Arguments:
- turns: bfloat16 [4096, 4, 1280], P(('groups', 'tm'), 'cuts', 'col'), parts along dimension 0, may hold values from -25 to 25
- shifts: int32 [8], P(('groups', 'tm')), parts along dimension 0, may hold values from -16 to 16
- bands: int32 [8], P(('groups', 'cuts')), parts along dimension 0, may hold values from 2 to 24
- memory: float32 [8], P(('groups', 'cuts')), parts along dimension 0, may hold values from 0.8 to 0.995
Outputs:
- filtered: bfloat16 [8192, 4, 1280], P(('groups', 'tm', 'col'), 'cuts'), parts along dimension 0
There are 2 independent parts, one for each index of `groups`. A program takes and returns all parts, laid end to end along the dimension named above; each array names one. Nothing has to cross between parts.
All inputs are finite; a program needn't handle non-finite values.
Results may differ from a plain program's by a relative error of at most 0.015.
The roundings to bfloat16 on the way count: a program that leaves them out, or rounds other values in their place, can miss the bound.
Values may be sent and summed in bfloat16 or wider, within the bound.
No kernel may reach another device: no remote copies, remote signals or barrier semaphores. Data moves between devices by JAX's collectives and lax.ppermute only.
A program may use at most 64 MiB of HBM per device.

v0:
```python
import math
import jax
import jax.numpy as jnp
from jax import lax
from jax.sharding import PartitionSpec as P

COLUMNS = 1280
BAND_FREQS = 64


def from_behind(block, axis, distance):
    devices = range(lax.axis_size(axis))
    route = [(i - distance, i) for i in devices if i - distance in devices]
    return lax.ppermute(block, axis, route)


def extended(shard, sides, width):
    for axis, dim in sides:
        devices, length = (lax.axis_size(axis), shard.shape[dim])
        up = [(i, (i + 1) % devices) for i in range(devices - 1)]
        down = [(j, i) for i, j in up]
        last = lax.slice_in_dim(shard, length - width, length, axis=dim)
        leading = lax.slice_in_dim(shard, 0, width, axis=dim)
        before = lax.ppermute(last, axis, up)
        after = lax.ppermute(leading, axis, down)
        shard = jnp.concatenate([before, shard, after], axis=dim)
    return shard


def wave_table(angle_count, freq_count):
    freq_index = lax.broadcasted_iota(jnp.int32, (freq_count, angle_count), 0) + 1
    angle_index = lax.broadcasted_iota(jnp.int32, (freq_count, angle_count), 1)
    phase_int = freq_index * angle_index % angle_count
    radians = phase_int.astype(jnp.float32) * (2.0 * math.pi / angle_count)
    return jnp.concatenate([jnp.cos(radians), jnp.sin(radians)], axis=0).astype(jnp.bfloat16)


def damping_weights(bands, freq_count, angle_count):
    freq_values = (jnp.arange(freq_count, dtype=jnp.int32) + 1).astype(jnp.float32)
    band_width = bands.astype(jnp.float32)
    gaussian = jnp.exp(-freq_values[:, None] ** 2 / (2.0 * band_width[None, :] ** 2)) * (
        2.0 / angle_count
    )
    return jnp.concatenate([gaussian, gaussian], axis=0)


def ramp_table(width_total, offset):
    source_col = lax.broadcasted_iota(jnp.int32, (width_total, width_total), 0)
    target_col = lax.broadcasted_iota(jnp.int32, (width_total, width_total), 1)
    lag_index = (target_col - source_col - offset) % width_total
    distance = jnp.minimum(lag_index, width_total - lag_index)
    dist_float = jnp.maximum(distance, 1).astype(jnp.float32)
    tap_value = jnp.where(
        distance == 0, 0.25, jnp.where(distance % 2 == 1, -1.0 / (math.pi**2 * dist_float**2), 0.0)
    )
    return tap_value.astype(jnp.bfloat16)


def local(turns, shifts, bands, memory):
    half_len, row_count, col_width = turns.shape
    angle_count = 2 * half_len
    spread = row_count * col_width
    wave_rows = wave_table(angle_count, BAND_FREQS)
    older_half = from_behind(turns, "tm", 1)
    flat_own = turns.reshape(half_len, spread)
    flat_old = older_half.reshape(half_len, spread)
    window = jnp.concatenate([flat_old, flat_own], axis=0)
    spectrum = jnp.dot(wave_rows, window, preferred_element_type=jnp.float32)
    column_sum = jnp.sum(window, axis=0, dtype=jnp.float32)
    profile = (column_sum / angle_count).reshape(row_count, col_width)
    decay_rate = memory.reshape(row_count, 1)
    tm_count = lax.axis_size("tm")
    tm_index = lax.axis_index("tm")
    lag_steps = tm_index - jnp.arange(tm_count, dtype=jnp.int32)
    lag_float = jnp.maximum(lag_steps, 0).astype(jnp.float32)
    powers = jnp.where(
        lag_steps[:, None] >= 0, jnp.power(decay_rate[:, 0][None, :], lag_float[:, None]), 0.0
    )
    weight = jnp.sum(powers, axis=0)[:, None]
    all_profiles = lax.all_gather(profile, "tm", axis=0, tiled=True)
    stacked = all_profiles.reshape(tm_count, row_count, col_width)
    weighted_sum = jnp.einsum("ur,urc->rc", powers, stacked, precision=lax.Precision.HIGHEST)
    estimate = weighted_sum / weight
    padded = extended(estimate, (("cuts", 0),), 1)
    smooth = (padded[:-2] + 2.0 * padded[1:-1] + padded[2:]) * 0.25
    weights = damping_weights(bands, BAND_FREQS, angle_count)
    scaled = (spectrum.reshape(2 * BAND_FREQS, row_count, col_width) * weights[:, :, None]).astype(
        jnp.bfloat16
    )
    low = jnp.dot(
        wave_rows.T, scaled.reshape(2 * BAND_FREQS, spread), preferred_element_type=jnp.float32
    )
    damped = (window - low - smooth.reshape(1, spread)).astype(jnp.bfloat16)
    damped = damped.reshape(angle_count, row_count, col_width)
    kernel = ramp_table(COLUMNS, shifts[0])
    row_block = lax.all_to_all(damped, "col", split_axis=0, concat_axis=2, tiled=True)
    lead_rows, item_count, full_width = row_block.shape
    result = jnp.dot(
        row_block.reshape(lead_rows * item_count, full_width),
        kernel,
        preferred_element_type=jnp.float32,
    )
    return result.reshape(lead_rows, item_count, full_width).astype(jnp.bfloat16)


def solution(mesh):
    placed = (
        P(("groups", "tm"), "cuts", "col"),
        P(("groups", "tm")),
        P(("groups", "cuts")),
        P(("groups", "cuts")),
    )
    return jax.shard_map(
        local,
        mesh=mesh,
        in_specs=placed,
        out_specs=P(("groups", "tm", "col"), "cuts", None),
        check_vma=False,
    )
```

profile of v0, /device:TPU:0, one launch (start us, length us, event | category | flops | bytes accessed | tf_op | source)
XLA Modules:
  0.0 95.9 jit_solution(11461236508998719598)
XLA Ops:
  0.0 0.0 copy-start.2
  0.0 5.2 %collective-permute-start = (bf16[512,2,640]{2,1,0:T(2,128)(2,1)}, bf16[512,2,640]{2,1,0:T(2,128)(2,1)S(1)}, u32[]{:S(2)}, u32[]{:S(2)}) collective-permute-start(bf16[512,2,640]{2,1,0:T(2,128)(2,1)} %param.4), channel_id=1, source_target_pairs={{0,4},{4,8},{8,12},{1,5},{5,9},{9,13},{2,6},{6,10},{10,14},{3,7},{... | collective-permute-start | bytes 3932168 | tf_op jit(solution)/shard_map/ppermute | solution.py:14
  5.2 2.6 %copy.17 = bf16[64,8,2,640]{3,1,2,0:T(8,128)(2,1)} copy(bf16[64,8,2,640]{3,2,1,0:T(2,128)(2,1)} %bitcast.30) | data formatting | bytes 2621440
  7.8 0.0 copy-done.2
  7.8 0.1 fusion.37
  7.9 0.0 copy-done.1
  7.9 0.2 fusion.49
  8.1 1.2 %cosine_convert_fusion = (bf16[64,1024]{1,0:T(8,128)(2,1)S(1)}, bf16[64,1024]{1,0:T(8,128)(2,1)S(1)}) fusion(s32[64]{0:T(128)S(1)} %iota_add_fusion), kind=kLoop, calls=%fused_computation.41 | loop fusion | flops 1048576 | bytes 262400 | tf_op jit(solution)/shard_map/convert
  9.3 24.1 %collective-permute-done = bf16[512,2,640]{2,1,0:T(2,128)(2,1)S(1)} collective-permute-done((bf16[512,2,640]{2,1,0:T(2,128)(2,1)}, bf16[512,2,640]{2,1,0:T(2,128)(2,1)S(1)}, u32[]{:S(2)}, u32[]{:S(2)}) %collective-permute-start) | collective-permute-done | bytes 1310752 | tf_op jit(solution)/shard_map/ppermute | solution.py:14
  33.4 0.2 copy.16
  33.6 0.1 constant_dynamic-update-slice_fusion.1
  33.7 1.0 %copy-done = bf16[64,8,2,640]{3,1,2,0:T(8,128)(2,1)S(1)} copy-done((bf16[64,8,2,640]{3,1,2,0:T(8,128)(2,1)S(1)}, bf16[64,8,2,640]{3,1,2,0:T(8,128)(2,1)}, u32[]{:S(2)}) %copy-start) | copy-done | bytes 1310744
  34.7 0.1 constant_dynamic-update-slice_fusion
  34.8 0.4 convert_reduce_fusion
  35.3 14.3 %all-gather = f32[4,2,640]{2,1,0:T(2,128)S(1)} all-gather(f32[1,2,640]{2,1,0:T(2,128)S(1)} %reshape.55), channel_id=1, replica_groups=mesh['groups'=2,'tm'=4,'cuts'=2,'col'=2] {'tm'}, dimensions={0}, use_global_device_ids=true | all-gather | bytes 25600 | tf_op jit(solution)/shard_map/all_gather | solution.py:80
  49.5 0.2 fusion.32
  49.7 0.1 bitcast_divide_fusion
  49.8 1.3 %collective-permute-start.2 = (f32[1,640]{1,0:T(1,128)S(1)}, f32[1,640]{1,0:T(1,128)}, u32[]{:S(2)}, u32[]{:S(2)}) collective-permute-start(f32[1,640]{1,0:T(1,128)S(1)} %get-tuple-element.8), channel_id=1, source_target_pairs={{2,0},{3,1},{6,4},{7,5},{10,8},{11,9},{14,12},{15,13},{18,16},{19,... | collective-permute-start | bytes 7688 | tf_op jit(solution)/shard_map/ppermute | solution.py:25
  51.1 5.7 %collective-permute-start.1 = (f32[1,640]{1,0:T(1,128)S(1)}, f32[1,640]{1,0:T(1,128)}, u32[]{:S(2)}, u32[]{:S(2)}) collective-permute-start(f32[1,640]{1,0:T(1,128)S(1)} %get-tuple-element.7), channel_id=1, source_target_pairs={{0,2},{1,3},{4,6},{5,7},{8,10},{9,11},{12,14},{13,15},{16,18},{17,... | collective-permute-start | bytes 7688 | tf_op jit(solution)/shard_map/ppermute | solution.py:24
  56.8 0.1 pad_maximum_fusion.2
  56.8 0.1 copy.10
  57.0 0.2 mul.58
  57.9 0.0 collective-permute-done.2
  57.9 0.0 collective-permute-done.1
  57.9 0.7 fusion.35
  58.6 2.7 %fusion.7 = bf16[1024,1280]{1,0:T(8,128)(2,1)} fusion(bf16[1024,1280]{1,0:T(8,128)(2,1)S(1)} %constant_dynamic-update-slice_fusion, f32[1280]{0:T(1024)S(1)} %sub.42, f32[128,1280]{1,0:T(8,128)S(1)} %bitcast.32, bf16[64,1024]{1,0:T(8,128)(2,1)S(1)} %get-tuple-element.10, bf16[64,1024]{1,0:T(8,128)(2,1)S(1)} %get-tuple-element.9), kind=kOutput, calls=%fused_computation.16 | convolution fusion | flops 677707776 | bytes 6165504 | tf_op jit(solution)/shard_map/dot_general | solution.py:90
  61.3 5.1 %reshape.54 = bf16[1024,2,640]{2,1,0:T(2,128)(2,1)S(1)} reshape(bf16[1024,1280]{1,0:T(8,128)(2,1)} %fusion.7) | data formatting | bytes 5242880 | tf_op jit(solution)/shard_map/reshape | solution.py:94
  66.4 5.8 %all_to_all.15 = bf16[1024,2,640]{2,1,0:T(2,128)(2,1)S(1)} all-to-all(bf16[1024,2,640]{2,1,0:T(2,128)(2,1)S(1)} %reshape.54), channel_id=1, replica_groups=mesh['groups'=2,'tm'=4,'cuts'=2,'col'=2] {'col'}, dimensions={0} | all-to-all | bytes 5242880 | tf_op jit(solution)/shard_map/all_to_all | solution.py:96
  72.2 2.7 %copy.23 = bf16[2,512,2,640]{3,0,1,2:T(2,128)(2,1)S(1)} copy(bf16[2,512,2,640]{3,2,1,0:T(2,128)(2,1)S(1)} %bitcast.25) | data formatting | bytes 5242880 | tf_op jit(solution)/shard_map/all_to_all | solution.py:96
  74.9 2.9 %dot_general.17 = bf16[512,2,1280]{2,0,1:T(8,128)(2,1)} reshape(bf16[512,2,2,640]{3,2,0,1:T(2,128)(2,1)S(1)} %bitcast.26) | data formatting | bytes 5242880 | tf_op jit(solution)/shard_map/dot_general | solution.py:98
  77.9 13.8 %convolution_convert_fusion = bf16[512,2,1280]{2,0,1:T(8,128)(2,1)S(1)} fusion(bf16[512,2,1280]{2,0,1:T(8,128)(2,1)} %dot_general.17, s32[]{:T(128)} %bitcast.24), kind=kOutput, calls=%fused_computation.17 | convolution fusion | flops 3407544320 | bytes 5242884 | tf_op jit(solution)/shard_map/dot_general | solution.py:98
  91.7 4.2 %copy.12 = bf16[512,2,1280]{2,1,0:T(2,128)(2,1)} copy(bf16[512,2,1280]{2,0,1:T(8,128)(2,1)S(1)} %convolution_convert_fusion) | data formatting | bytes 5242880 | tf_op jit(solution)/shard_map/convert_element_type | solution.py:103
  (12 shorter events, 0.1 us)
Async XLA Ops:
  0.0 7.8 %copy-start.2 = (s32[2]{0:T(128)S(1)}, s32[2]{0:T(128)}, u32[]{:S(2)}) copy-start(s32[2]{0:T(128)} %param.6) | copy-start | bytes 28
  0.0 7.9 %copy-start.1 = (f32[2]{0:T(128)S(1)}, f32[2]{0:T(128)}, u32[]{:S(2)}) copy-start(f32[2]{0:T(128)} %param.7) | copy-start | bytes 28
  0.0 33.4 %collective-permute-start = (bf16[512,2,640]{2,1,0:T(2,128)(2,1)}, bf16[512,2,640]{2,1,0:T(2,128)(2,1)S(1)}, u32[]{:S(2)}, u32[]{:S(2)}) collective-permute-start(bf16[512,2,640]{2,1,0:T(2,128)(2,1)} %param.4), channel_id=1, source_target_pairs={{0,4},{4,8},{8,12},{1,5},{5,9},{9,13},{2,6},{6,10},{10,14},{3,7},{... | collective-permute-start | bytes 3932168 | tf_op jit(solution)/shard_map/ppermute | solution.py:14
  33.4 1.3 %copy-start = (bf16[64,8,2,640]{3,1,2,0:T(8,128)(2,1)S(1)}, bf16[64,8,2,640]{3,1,2,0:T(8,128)(2,1)}, u32[]{:S(2)}) copy-start(bf16[64,8,2,640]{3,1,2,0:T(8,128)(2,1)} %copy.17) | copy-start | bytes 3932164
  49.8 8.1 %collective-permute-start.2 = (f32[1,640]{1,0:T(1,128)S(1)}, f32[1,640]{1,0:T(1,128)}, u32[]{:S(2)}, u32[]{:S(2)}) collective-permute-start(f32[1,640]{1,0:T(1,128)S(1)} %get-tuple-element.8), channel_id=1, source_target_pairs={{2,0},{3,1},{6,4},{7,5},{10,8},{11,9},{14,12},{15,13},{18,16},{19,... | collective-permute-start | bytes 7688 | tf_op jit(solution)/shard_map/ppermute | solution.py:25
  51.1 6.8 %collective-permute-start.1 = (f32[1,640]{1,0:T(1,128)S(1)}, f32[1,640]{1,0:T(1,128)}, u32[]{:S(2)}, u32[]{:S(2)}) collective-permute-start(f32[1,640]{1,0:T(1,128)S(1)} %get-tuple-element.7), channel_id=1, source_target_pairs={{0,2},{1,3},{4,6},{5,7},{8,10},{9,11},{12,14},{13,15},{16,18},{17,... | collective-permute-start | bytes 7688 | tf_op jit(solution)/shard_map/ppermute | solution.py:24
where the time goes:
time: 96.3 us; the launch traced here: 95.9 us
  waiting for transfers between devices  24.1 us (25%)
  blocking collectives  20.1 us (21%)
  local copies, waits for them, and re-layouts  19.3 us (20%)
  matrix products  16.6 us (17%)
  starting transfers between devices  12.1 us (13%)
  other arithmetic  2.81 us (3%)
    ppermute x1, waiting for transfers between devices, from_behind(): return lax.ppermute(block, axis, route)  24.1 us
    all_gather x1, blocking collectives, local(): all_profiles = lax.all_gather(profile, 'tm', axis=0, tiled=True)  14.3 us
    dot_general x1, matrix products, local(): jnp.dot(row_block.reshape(lead_rows * item_count, full_width), kernel, pr...  13.8 us
    all_to_all x1, blocking collectives, local(): lax.all_to_all(damped, 'col', split_axis=0, concat_axis=2, tiled=True)  5.84 us
    ppermute x1, starting transfers between devices, extended(): before = lax.ppermute(last, axis, up)  5.68 us
    ppermute x1, starting transfers between devices, from_behind(): return lax.ppermute(block, axis, route)  5.16 us
    reshape x1, local copies, waits for them, and re-layouts, local(): damped = damped.reshape(angle_count, row_count, col_width)  5.07 us
    convert_element_type x1, local copies, waits for them, and re-layouts, local(): result.reshape(lead_rows, item_count, full_width).astype(jnp.bfloat16)  4.19 us
  transfers between devices with their start and end apart: 3, of which 1 were waited for; matrix products, arithmetic and copies ran while one was open for 5% of the time, Pallas kernels for 0%

commit v1 on v0

--- a/solution.py
+++ b/solution.py
@@ -93,7 +93,11 @@
     damped = (window - low - smooth.reshape(1, spread)).astype(jnp.bfloat16)
     damped = damped.reshape(angle_count, row_count, col_width)
     kernel = ramp_table(COLUMNS, shifts[0])
-    row_block = lax.all_to_all(damped, "col", split_axis=0, concat_axis=2, tiled=True)
+    reached = lax.axis_size("col")
+    z1 = jnp.split(damped, reached, 0)
+    found_now = jnp.stack(z1, axis=0)
+    piece_now = lax.all_to_all(found_now, split_axis=0, axis_name="col", concat_axis=0)
+    row_block = jnp.concatenate(piece_now, 2)
     lead_rows, item_count, full_width = row_block.shape
     result = jnp.dot(
         row_block.reshape(lead_rows * item_count, full_width),

time: 96.3 us -> 104 us (1.080)
  other arithmetic: 2.81 us -> 8.06 us
  local copies, waits for them, and re-layouts: 19.3 us -> 21.4 us
    another operation x1 -> x2, other arithmetic: 1.23 us -> 6.47 us  [the longest x1 5.24 us: local(): found_now = jnp.stack(z1, axis=0)]
    another operation x0 -> x2, local copies, waits for them, and re-layouts: none -> 4.19 us  [local(): found_now = jnp.stack(z1, axis=0)]
    split x0 -> x1, local copies, waits for them, and re-layouts: none -> 2.95 us  [local(): z1 = jnp.split(damped, reached, 0)]
    all_to_all x1 -> x0, local copies, waits for them, and re-layouts: 2.7 us -> none  [local(): lax.all_to_all(damped, 'col', split_axis=0, concat_axis=2, tiled=True)]
    reshape x1, local copies, waits for them, and re-layouts: 5.07 us -> 2.7 us  [local(): row_block = jnp.concatenate(piece_now, 2)]
  transfers between devices with their start and end apart: 3 -> 3, of which waited for: 1 -> 1; matrix products, arithmetic and copies ran while one was open for 5% -> 4% of each run, Pallas kernels for 0% -> 0%
where the time goes in v1:
time: 104 us; the launch traced here: 103 us
  waiting for transfers between devices  24.1 us (23%)
  local copies, waits for them, and re-layouts  21.4 us (21%)
  blocking collectives  20.1 us (19%)
  matrix products  16.6 us (16%)
  starting transfers between devices  12.2 us (12%)
  other arithmetic  8.06 us (8%)
    ppermute x1, waiting for transfers between devices, from_behind(): return lax.ppermute(block, axis, route)  24.1 us
    all_gather x1, blocking collectives, local(): all_profiles = lax.all_gather(profile, 'tm', axis=0, tiled=True)  14.3 us
    dot_general x1, matrix products, local(): jnp.dot(row_block.reshape(lead_rows * item_count, full_width), kernel, pr...  13.8 us
    all_to_all x1, blocking collectives, local(): lax.all_to_all(found_now, split_axis=0, axis_name='col', concat_axis=0)  5.84 us
    ppermute x1, starting transfers between devices, extended(): before = lax.ppermute(last, axis, up)  5.71 us
    another operation x1, other arithmetic, local(): found_now = jnp.stack(z1, axis=0)  5.24 us
    ppermute x1, starting transfers between devices, from_behind(): return lax.ppermute(block, axis, route)  5.16 us
    another operation x2, local copies, waits for them, and re-layouts, local(): found_now = jnp.stack(z1, axis=0)  4.19 us
  transfers between devices with their start and end apart: 3, of which 1 were waited for; matrix products, arithmetic and copies ran while one was open for 4% of the time, Pallas kernels for 0%

profile of v1, /device:TPU:0, one launch (start us, length us, event | category | flops | bytes accessed | tf_op | source)
XLA Modules:
  0.0 103.2 jit_solution(11423649982785886773)
XLA Ops:
  0.0 5.2 %collective-permute-start = (bf16[512,2,640]{2,1,0:T(2,128)(2,1)}, bf16[512,2,640]{2,1,0:T(2,128)(2,1)S(1)}, u32[]{:S(2)}, u32[]{:S(2)}) collective-permute-start(bf16[512,2,640]{2,1,0:T(2,128)(2,1)} %param.4), channel_id=1, source_target_pairs={{0,4},{4,8},{8,12},{1,5},{5,9},{9,13},{2,6},{6,10},{10,14},{3,7},{... | collective-permute-start | bytes 3932168 | tf_op jit(solution)/shard_map/ppermute | solution.py:14
  5.2 2.6 %copy.17 = bf16[64,8,2,640]{3,1,2,0:T(8,128)(2,1)} copy(bf16[64,8,2,640]{3,2,1,0:T(2,128)(2,1)} %bitcast.26) | data formatting | bytes 2621440
  7.8 0.1 fusion.37
  7.9 0.2 fusion.49
  8.1 1.2 %cosine_convert_fusion = (bf16[64,1024]{1,0:T(8,128)(2,1)S(1)}, bf16[64,1024]{1,0:T(8,128)(2,1)S(1)}) fusion(s32[64]{0:T(128)S(1)} %iota_add_fusion), kind=kLoop, calls=%fused_computation.41 | loop fusion | flops 1048576 | bytes 262400 | tf_op jit(solution)/shard_map/convert
  9.3 24.1 %collective-permute-done = bf16[512,2,640]{2,1,0:T(2,128)(2,1)S(1)} collective-permute-done((bf16[512,2,640]{2,1,0:T(2,128)(2,1)}, bf16[512,2,640]{2,1,0:T(2,128)(2,1)S(1)}, u32[]{:S(2)}, u32[]{:S(2)}) %collective-permute-start) | collective-permute-done | bytes 1310752 | tf_op jit(solution)/shard_map/ppermute | solution.py:14
  33.4 0.2 copy.16
  33.6 0.1 constant_dynamic-update-slice_fusion.1
  33.7 1.0 copy-done
  34.7 0.1 constant_dynamic-update-slice_fusion
  34.8 0.4 convert_reduce_fusion
  35.3 14.3 %all-gather = f32[4,2,640]{2,1,0:T(2,128)S(1)} all-gather(f32[1,2,640]{2,1,0:T(2,128)S(1)} %reshape.58), channel_id=1, replica_groups=mesh['groups'=2,'tm'=4,'cuts'=2,'col'=2] {'tm'}, dimensions={0}, use_global_device_ids=true | all-gather | bytes 25600 | tf_op jit(solution)/shard_map/all_gather | solution.py:80
  49.5 0.2 fusion.32
  49.7 0.1 bitcast_divide_fusion
  49.8 1.3 %collective-permute-start.2 = (f32[1,640]{1,0:T(1,128)S(1)}, f32[1,640]{1,0:T(1,128)}, u32[]{:S(2)}, u32[]{:S(2)}) collective-permute-start(f32[1,640]{1,0:T(1,128)S(1)} %get-tuple-element.10), channel_id=1, source_target_pairs={{2,0},{3,1},{6,4},{7,5},{10,8},{11,9},{14,12},{15,13},{18,16},{19,... | collective-permute-start | bytes 7688 | tf_op jit(solution)/shard_map/ppermute | solution.py:25
  51.1 5.7 %collective-permute-start.1 = (f32[1,640]{1,0:T(1,128)S(1)}, f32[1,640]{1,0:T(1,128)}, u32[]{:S(2)}, u32[]{:S(2)}) collective-permute-start(f32[1,640]{1,0:T(1,128)S(1)} %get-tuple-element.9), channel_id=1, source_target_pairs={{0,2},{1,3},{4,6},{5,7},{8,10},{9,11},{12,14},{13,15},{16,18},{17,... | collective-permute-start | bytes 7688 | tf_op jit(solution)/shard_map/ppermute | solution.py:24
  56.8 0.1 pad_maximum_fusion.3
  56.9 0.1 copy.10
  57.0 0.2 mul.58
  57.9 0.0 collective-permute-done.2
  57.9 0.0 collective-permute-done.1
  57.9 0.7 fusion.35
  58.7 2.7 %fusion.7 = bf16[1024,1280]{1,0:T(8,128)(2,1)} fusion(bf16[1024,1280]{1,0:T(8,128)(2,1)S(1)} %constant_dynamic-update-slice_fusion, f32[1280]{0:T(1024)S(1)} %sub.42, f32[128,1280]{1,0:T(8,128)S(1)} %bitcast.28, bf16[64,1024]{1,0:T(8,128)(2,1)S(1)} %get-tuple-element.12, bf16[64,1024]{1,0:T(8,128)(2,1)S(1)} %get-tuple-element.11), kind=kOutput, calls=%fused_computation.16 | convolution fusion | flops 677707776 | bytes 6165504 | tf_op jit(solution)/shard_map/dot_general | solution.py:90
  61.4 3.0 %fusion.50 = (bf16[512,1280]{1,0:T(8,128)(2,1)S(1)}, bf16[512,1280]{1,0:T(8,128)(2,1)}) fusion(bf16[1024,1280]{1,0:T(8,128)(2,1)} %fusion.7), kind=kLoop, calls=%fused_computation.76 | loop fusion | bytes 5242880 | tf_op jit(solution)/shard_map/split | solution.py:97
  64.3 3.0 %stack.10 = bf16[1,512,2,640]{3,2,1,0:T(2,128)(2,1)S(1)} reshape(bf16[512,1280]{1,0:T(8,128)(2,1)} %get-tuple-element.8) | data formatting | bytes 2621440 | tf_op jit(solution)/shard_map/stack | solution.py:98
  67.3 1.2 %stack.9 = bf16[1,512,2,640]{3,2,1,0:T(2,128)(2,1)} reshape(bf16[512,1280]{1,0:T(8,128)(2,1)S(1)} %get-tuple-element.7) | data formatting | bytes 2621440 | tf_op jit(solution)/shard_map/stack | solution.py:98
  68.5 5.2 %pad_maximum_fusion = bf16[2,512,2,640]{3,2,1,0:T(2,128)(2,1)S(1)} fusion(bf16[1,512,2,640]{3,2,1,0:T(2,128)(2,1)S(1)} %stack.10, bf16[1,512,2,640]{3,2,1,0:T(2,128)(2,1)} %stack.9), kind=kLoop, calls=%fused_computation.28 | loop fusion | flops 1310720 | bytes 5242880 | tf_op jit(solution)/shard_map/stack | solution.py:98
  73.8 5.8 %all_to_all.5 = bf16[2,512,2,640]{3,2,1,0:T(2,128)(2,1)S(1)} all-to-all(bf16[2,512,2,640]{3,2,1,0:T(2,128)(2,1)S(1)} %pad_maximum_fusion), channel_id=1, replica_groups=mesh['groups'=2,'tm'=4,'cuts'=2,'col'=2] {'col'}, dimensions={0} | all-to-all | bytes 5242880 | tf_op jit(solution)/shard_map/all_to_all | solution.py:99
  79.6 2.7 %copy.11 = bf16[512,2,2,640]{3,2,0,1:T(2,128)(2,1)S(1)} copy(bf16[512,2,2,640]{3,1,0,2:T(2,128)(2,1)S(1)} %bitcast.22) | data formatting | bytes 5242880 | tf_op jit(solution)/shard_map/reshape | solution.py:100
  82.3 2.9 %dot_general.17 = bf16[512,2,1280]{2,0,1:T(8,128)(2,1)} reshape(bf16[512,2,2,640]{3,2,0,1:T(2,128)(2,1)S(1)} %copy.11) | data formatting | bytes 5242880 | tf_op jit(solution)/shard_map/dot_general | solution.py:102
  85.3 13.8 %convolution_convert_fusion = bf16[512,2,1280]{2,0,1:T(8,128)(2,1)S(1)} fusion(bf16[512,2,1280]{2,0,1:T(8,128)(2,1)} %dot_general.17, s32[]{:T(128)} %bitcast.21), kind=kOutput, calls=%fused_computation.17 | convolution fusion | flops 3407544320 | bytes 5242884 | tf_op jit(solution)/shard_map/dot_general | solution.py:102
  99.0 4.2 %copy.12 = bf16[512,2,1280]{2,1,0:T(2,128)(2,1)} copy(bf16[512,2,1280]{2,0,1:T(8,128)(2,1)S(1)} %convolution_convert_fusion) | data formatting | bytes 5242880 | tf_op jit(solution)/shard_map/convert_element_type | solution.py:107
  (15 shorter events, 0.1 us)
Async XLA Ops:
  0.0 7.8 %copy-start.2 = (s32[2]{0:T(128)S(1)}, s32[2]{0:T(128)}, u32[]{:S(2)}) copy-start(s32[2]{0:T(128)} %param.6) | copy-start | bytes 28
  0.0 7.9 %copy-start.1 = (f32[2]{0:T(128)S(1)}, f32[2]{0:T(128)}, u32[]{:S(2)}) copy-start(f32[2]{0:T(128)} %param.7) | copy-start | bytes 28
  0.0 33.4 %collective-permute-start = (bf16[512,2,640]{2,1,0:T(2,128)(2,1)}, bf16[512,2,640]{2,1,0:T(2,128)(2,1)S(1)}, u32[]{:S(2)}, u32[]{:S(2)}) collective-permute-start(bf16[512,2,640]{2,1,0:T(2,128)(2,1)} %param.4), channel_id=1, source_target_pairs={{0,4},{4,8},{8,12},{1,5},{5,9},{9,13},{2,6},{6,10},{10,14},{3,7},{... | collective-permute-start | bytes 3932168 | tf_op jit(solution)/shard_map/ppermute | solution.py:14
  33.4 1.3 %copy-start = (bf16[64,8,2,640]{3,1,2,0:T(8,128)(2,1)S(1)}, bf16[64,8,2,640]{3,1,2,0:T(8,128)(2,1)}, u32[]{:S(2)}) copy-start(bf16[64,8,2,640]{3,1,2,0:T(8,128)(2,1)} %copy.17) | copy-start | bytes 3932164
  49.8 8.1 %collective-permute-start.2 = (f32[1,640]{1,0:T(1,128)S(1)}, f32[1,640]{1,0:T(1,128)}, u32[]{:S(2)}, u32[]{:S(2)}) collective-permute-start(f32[1,640]{1,0:T(1,128)S(1)} %get-tuple-element.10), channel_id=1, source_target_pairs={{2,0},{3,1},{6,4},{7,5},{10,8},{11,9},{14,12},{15,13},{18,16},{19,... | collective-permute-start | bytes 7688 | tf_op jit(solution)/shard_map/ppermute | solution.py:25
  51.1 6.9 %collective-permute-start.1 = (f32[1,640]{1,0:T(1,128)S(1)}, f32[1,640]{1,0:T(1,128)}, u32[]{:S(2)}, u32[]{:S(2)}) collective-permute-start(f32[1,640]{1,0:T(1,128)S(1)} %get-tuple-element.9), channel_id=1, source_target_pairs={{0,2},{1,3},{4,6},{5,7},{8,10},{9,11},{12,14},{13,15},{16,18},{17,... | collective-permute-start | bytes 7688 | tf_op jit(solution)/shard_map/ppermute | solution.py:24
